TPU v7x, 32 devices: a whole 2x2x4 slice. The times are simulated.
32 devices in a mesh: ctx: 8 (over z, y), head: 4 (over x, core).
Axes of the slice: x: 2, y: 2, z: 4, core: 2. Of those that a mesh axis runs over, the one named last changes fastest.
Arguments:
- queries: bfloat16 [4096, 2048], P(('ctx', 'head')), may hold values from -6 to 6
- key_rows: bfloat16 [4096, 256], P(('ctx', 'head')), may hold values from -6 to 6
- value_rows: bfloat16 [4096, 256], P(('ctx', 'head')), may hold values from -8 to 8
- group_kv_head: int32 [4], replicated, may hold values from 0 to 1, as said below
- doc_ids: int32 [4096], replicated, may hold values from 0 to 127, never falling along the last dimension, each value on 1 to 64 neighbouring positions
Outputs:
- attended: bfloat16 [4096, 2048], P(('ctx', 'head'))
Inputs may be any that keep to these rules, and one draw needn't show every extreme that they name: `group_kv_head`: each key-value head is named by exactly two groups. `doc_ids`: ids never fall along the sequence and every id appears; a document holds at most 64 tokens, and one holds exactly that many.
All inputs are finite; a program needn't handle non-finite values.
Results may differ from a plain program's by a relative error of at most 0.0027.
Values may be sent and summed in bfloat16 or wider, within the bound.
No kernel may reach another device: no remote copies, remote signals or barrier semaphores. Data moves between devices by JAX's collectives and lax.ppermute only.
A program may use at most 64 MiB of HBM per device.

v0:
```python
import math
import jax
import jax.numpy as jnp
from jax import lax
from jax.sharding import PartitionSpec as P

HEAD_DIM = 128
HEADS_DEV = 4
neg_fill = -1e30


def passed_along(array, axis, by):
    peers = lax.axis_size(axis)
    pairs = [(i, i + by) for i in range(peers) if 0 <= i + by < peers]
    return lax.ppermute(array, axis, pairs)


def from_partner(array, axis, stride):
    return lax.ppermute(array, axis, [(i, i ^ 1 << stride) for i in range(lax.axis_size(axis))])


def attend(query_tile, key_window, value_window, query_pos, query_doc, key_pos, key_doc):
    scale_factor = 1.0 / math.sqrt(query_tile.shape[3])
    visible = (key_pos[:, None, :] <= query_pos[:, :, None]) & (
        key_doc[:, None, :] == query_doc[:, :, None]
    )
    results = []
    for head_index in range(query_tile.shape[2]):
        scores = (
            jnp.einsum(
                "nhs,nos->nho",
                query_tile[:, :, head_index],
                key_window,
                preferred_element_type=jnp.float32,
            )
            * scale_factor
        )
        scores = jnp.where(visible, scores, neg_fill)
        peak = jnp.max(scores, axis=2, keepdims=True)
        expo = jnp.where(visible, jnp.exp(scores - peak), 0.0)
        totals = jnp.sum(expo, axis=2, keepdims=True)
        mixed = jnp.einsum(
            "fkm,fmp->fkp",
            expo.astype(jnp.bfloat16),
            value_window,
            preferred_element_type=jnp.float32,
        )
        results.append((mixed / totals).astype(jnp.bfloat16))
    return jnp.concatenate(results, axis=2)


def three_tiles(values, tile_count, tile):
    stacked = values.reshape((tile_count + 2, tile) + values.shape[1:])
    return jnp.concatenate([stacked[:tile_count], stacked[1 : tile_count + 1], stacked[2:]], axis=1)


def on_device(queries, key_rows, value_rows, group_kv_head, doc_ids):
    head_count = lax.axis_size("head")
    local_rows = queries.shape[0]
    kv_count = key_rows.shape[1] // HEAD_DIM
    width = HEADS_DEV * HEAD_DIM
    half_dim = HEAD_DIM // 2
    grouped = queries.reshape(local_rows, head_count, width)
    key_split = key_rows.reshape(local_rows, kv_count, HEAD_DIM)
    value_split = value_rows.reshape(local_rows, kv_count, HEAD_DIM)
    tok_dev = local_rows * head_count
    reach = tok_dev // 8
    tile = tok_dev // 16
    tile_count = 16
    order = jnp.argsort(group_kv_head, stable=True)
    reorder = (order[:, None] == jnp.arange(head_count, dtype=jnp.int32)[None, :]).astype(
        jnp.bfloat16
    )
    grouped = jnp.einsum(
        "sg,rgw->rsw", reorder, grouped, preferred_element_type=jnp.float32
    ).astype(jnp.bfloat16)
    key_parts = key_split.reshape(local_rows, kv_count * 2, half_dim)
    value_parts = value_split.reshape(local_rows, kv_count * 2, half_dim)
    pieces = jnp.concatenate([key_parts, value_parts], axis=2)
    local_queries, local_pieces = (
        lax.all_to_all(grouped, "head", split_axis=1, concat_axis=0, tiled=True),
        lax.all_to_all(pieces, "head", split_axis=1, concat_axis=0, tiled=True),
    )
    own_pieces = local_pieces.reshape(tok_dev, HEAD_DIM)
    rim = passed_along(own_pieces[tok_dev - reach :], "ctx", 1)
    mine = jnp.concatenate([rim, own_pieces], axis=0)
    partner = from_partner(mine, "head", 0)
    lower = lax.axis_index("head") % 2 == 0
    own_key = mine[:, :half_dim]
    own_value = mine[:, half_dim:]
    other_key = partner[:, :half_dim]
    other_value = partner[:, half_dim:]
    key_all = jnp.where(
        lower,
        jnp.concatenate([own_key, other_key], axis=1),
        jnp.concatenate([other_key, own_key], axis=1),
    )
    value_all = jnp.where(
        lower,
        jnp.concatenate([own_value, other_value], axis=1),
        jnp.concatenate([other_value, own_value], axis=1),
    )
    query_tiles = local_queries.reshape(tile_count, tile, HEADS_DEV, HEAD_DIM)
    block_start = lax.axis_index("ctx") * tok_dev
    doc_pad = jnp.concatenate([jnp.full((reach,), -1, jnp.int32), doc_ids], axis=0)
    key_doc = lax.dynamic_slice_in_dim(doc_pad, block_start, reach + tok_dev, 0)
    query_doc = lax.dynamic_slice_in_dim(doc_ids, block_start, tok_dev, 0).reshape(tile_count, tile)
    key_pos = block_start - reach + jnp.arange(reach + tok_dev, dtype=jnp.int32)
    query_pos = (block_start + jnp.arange(tok_dev, dtype=jnp.int32)).reshape(tile_count, tile)
    key_windows = three_tiles(key_all, tile_count, tile)
    value_windows = three_tiles(value_all, tile_count, tile)
    key_doc_windows = three_tiles(key_doc, tile_count, tile)
    key_pos_windows = three_tiles(key_pos, tile_count, tile)
    result = attend(
        query_tiles,
        key_windows,
        value_windows,
        query_pos,
        query_doc,
        key_pos_windows,
        key_doc_windows,
    )
    result = result.reshape(tok_dev, 1, width)
    returned = lax.all_to_all(result, "head", split_axis=0, concat_axis=1, tiled=True)
    returned = jnp.einsum(
        "sg,rsw->rgw", reorder, returned, preferred_element_type=jnp.float32
    ).astype(jnp.bfloat16)
    return returned.reshape(local_rows, head_count * width)


def solution(mesh):
    placed = (
        P(("ctx", "head"), None),
        P(("ctx", "head"), None),
        P(("ctx", "head"), None),
        P(),
        P(),
    )
    return jax.shard_map(
        on_device, mesh=mesh, in_specs=placed, out_specs=P(("ctx", "head"), None), check_vma=False
    )
```

profile of v0, /device:TPU:0, one launch (start us, length us, event | category | flops | bytes accessed | tf_op | source)
XLA Modules:
  0.0 51.2 jit_solution(3134931440906846333)
XLA Ops:
  0.0 1.0 %copy.31 = bf16[128,256]{0,1:T(8,128)(2,1)S(1)} copy(bf16[128,256]{1,0:T(8,128)(2,1)} %param.7) | data formatting | bytes 131072 | tf_op args[2]
  1.0 0.1 copy.30
  1.1 0.7 %pad_maximum_fusion.4 = bf16[128,4,128]{0,2,1:T(8,128)(2,1)} fusion(bf16[128,4,64]{0,2,1:T(8,128)(2,1)S(1)} %bitcast.77, bf16[128,4,64]{0,2,1:T(8,128)(2,1)S(1)} %bitcast.78), kind=kLoop, calls=%fused_computation.48 | loop fusion | flops 262144 | bytes 262144 | tf_op jit(solution)/shard_map/concatenate | solution.py:79
  1.8 4.2 %all-to-all-start.1 = ((bf16[128,4,128]{0,2,1:T(8,128)(2,1)}), bf16[128,4,128]{0,2,1:T(8,128)(2,1)S(1)}, u32[]{:S(2)}, u32[]{:S(2)}) async-start(bf16[128,4,128]{0,2,1:T(8,128)(2,1)} %pad_maximum_fusion.4), calls=%async_computation.1 | async-start | bytes 262144 | tf_op jit(solution)/shard_map/all_to_all | solution.py:82
  6.0 0.4 reshape.83
  6.5 0.6 %copy-done.3 = s32[4]{0:T(128)S(1)} copy-done((s32[4]{0:T(128)S(1)}, s32[4]{0:T(128)}, u32[]{:S(2)}) %copy-start.3) | copy-done | bytes 40
  7.1 0.7 %sort.17 = (s32[4]{0:T(128)}, s32[4]{0:T(128)S(1)}) sort(s32[4]{0:T(128)S(1)} %copy-done.3, s32[4]{0:T(128)S(1)} %iota.54), dimensions={0}, to_apply=%region_0.0 | sort | flops 8 | bytes 64 | tf_op jit(solution)/shard_map/jit(argsort)/sort | solution.py:70
  7.9 0.5 %fusion.4 = bf16[128,4,512]{2,1,0:T(4,128)(2,1)S(1)} fusion(bf16[128,4,512]{2,1,0:T(4,128)(2,1)S(1)} %reshape.83, s32[4]{0:T(128)S(1)} %get-tuple-element.6), kind=kOutput, calls=%fused_computation.6 | convolution fusion | flops 2359312 | bytes 1048592 | tf_op jit(solution)/shard_map/sg,rgw->rsw/dot_general | solution.py:74
  8.4 0.2 copy-done.2
  8.6 0.1 pad_dynamic-slice_fusion
  8.7 0.9 %copy.28 = bf16[128,4,512]{2,0,1:T(8,128)(2,1)} copy(bf16[128,4,512]{2,1,0:T(4,128)(2,1)S(1)} %fusion.4) | data formatting | bytes 1048576 | tf_op jit(solution)/shard_map/convert_element_type | solution.py:76
  9.6 0.1 slice.128
  9.7 0.1 slice.126
  9.8 0.8 %all-to-all-done.1 = bf16[128,4,128]{0,2,1:T(8,128)(2,1)S(1)} async-done(((bf16[128,4,128]{0,2,1:T(8,128)(2,1)}), bf16[128,4,128]{0,2,1:T(8,128)(2,1)S(1)}, u32[]{:S(2)}, u32[]{:S(2)}) %all-to-all-start.1) | async-done | bytes 131104 | tf_op jit(solution)/shard_map/all_to_all | solution.py:82
  10.6 3.5 %all-to-all-start = ((bf16[128,4,512]{2,0,1:T(8,128)(2,1)}), bf16[128,4,512]{2,0,1:T(8,128)(2,1)S(1)}, u32[]{:S(2)}, u32[]{:S(2)}) async-start(bf16[128,4,512]{2,0,1:T(8,128)(2,1)} %copy.28), calls=%async_computation | async-start | bytes 1048576 | tf_op jit(solution)/shard_map/all_to_all | solution.py:81
  14.1 0.1 copy.32
  14.3 4.0 %collective-permute-start = (bf16[64,128]{1,0:T(8,128)(2,1)S(1)}, bf16[64,128]{1,0:T(8,128)(2,1)S(1)}, u32[]{:S(2)}, u32[]{:S(2)}) collective-permute-start(bf16[64,128]{1,0:T(8,128)(2,1)S(1)} %slice.154), channel_id=1, source_target_pairs={{0,4},{4,8},{8,12},{12,16},{16,20},{20,24},{24,28},{1,5},{5,9},{9,... | collective-permute-start | bytes 49160 | tf_op jit(solution)/shard_map/ppermute | solution.py:15
  18.2 0.1 pad_add_fusion
  18.3 1.3 %collective-permute-done = bf16[64,128]{1,0:T(8,128)(2,1)S(1)} collective-permute-done((bf16[64,128]{1,0:T(8,128)(2,1)S(1)}, bf16[64,128]{1,0:T(8,128)(2,1)S(1)}, u32[]{:S(2)}, u32[]{:S(2)}) %collective-permute-start) | collective-permute-done | bytes 16416 | tf_op jit(solution)/shard_map/ppermute | solution.py:15
  19.8 0.1 dynamic_slice.7
  19.9 0.1 eq.34
  19.9 0.1 fusion.28
  20.1 1.1 %collective-permute-done.1 = bf16[576,128]{1,0:T(8,128)(2,1)S(1)} collective-permute-done((bf16[576,128]{1,0:T(8,128)(2,1)S(1)}, bf16[576,128]{1,0:T(8,128)(2,1)S(1)}, u32[]{:S(2)}, u32[]{:S(2)}) %collective-permute-start.1) | collective-permute-done | bytes 147488 | tf_op jit(solution)/shard_map/ppermute | solution.py:19
  21.1 0.1 fusion.48
  21.2 0.3 maximum_select_fusion
  21.7 1.2 %all-to-all-done = bf16[128,4,512]{2,0,1:T(8,128)(2,1)S(1)} async-done(((bf16[128,4,512]{2,0,1:T(8,128)(2,1)}), bf16[128,4,512]{2,0,1:T(8,128)(2,1)S(1)}, u32[]{:S(2)}, u32[]{:S(2)}) %all-to-all-start) | async-done | bytes 524320 | tf_op jit(solution)/shard_map/all_to_all | solution.py:81
  22.9 0.1 reshape.84
  23.0 1.1 %fusion.46 = (bf16[16,32,1,128]{3,2,1,0:T(2,128)(2,1)S(1)}, bf16[16,32,1,128]{3,2,1,0:T(2,128)(2,1)S(1)}, bf16[16,32,1,128]{3,2,1,0:T(2,128)(2,1)S(1)}, bf16[16,32,1,128]{3,2,1,0:T(2,128)(2,1)S(1)}) fusion(bf16[16,32,4,128]{3,2,1,0:T(4,128)(2,1)S(1)} %reshape.84), kind=kLoop, calls=%fused_computation.74 | loop fusion | bytes 1048576 | tf_op jit(solution)/shard_map/slice | solution.py:32
  24.2 1.4 %fusion.52 = f32[16,32]{1,0:T(8,128)S(1)} fusion(bf16[16,32,1,128]{3,2,1,0:T(2,128)(2,1)S(1)} %get-tuple-element.10, bf16[16,32,128]{2,1,0:T(8,128)(2,1)S(1)} %bitcast.99, bf16[16,32,128]{2,1,0:T(8,128)(2,1)S(1)} %bitcast.107, bf16[16,32,128]{2,1,0:T(8,128)(2,1)S(1)} %bitcast.91, s32[16,32]{1,0:T(8,128)S(1)} %eq.34, s32[16,96]{1,0:T(8,128)S(1)} %get-tuple-element.30, ...), kind=kOutput, calls=%fused_computation.80 | convolution fusion | flops 14303327 | bytes 542720 | tf_op jit(solution)/shard_map/sub | solution.py:40
  25.5 0.5 fusion.9
  26.0 1.4 %fusion.53 = f32[16,32]{1,0:T(8,128)S(1)} fusion(bf16[16,32,1,128]{3,2,1,0:T(2,128)(2,1)S(1)} %get-tuple-element.8, bf16[16,32,128]{2,1,0:T(8,128)(2,1)S(1)} %bitcast.101, bf16[16,32,128]{2,1,0:T(8,128)(2,1)S(1)} %bitcast.109, bf16[16,32,128]{2,1,0:T(8,128)(2,1)S(1)} %bitcast.93, s32[16,32]{1,0:T(8,128)S(1)} %eq.34, s32[16,96]{1,0:T(8,128)S(1)} %get-tuple-element.30, ...), kind=kOutput, calls=%fused_computation.81 | convolution fusion | flops 14303327 | bytes 542720 | tf_op jit(solution)/shard_map/sub | solution.py:40
  27.4 0.5 fusion.10
  27.9 1.4 %fusion.54 = f32[16,32]{1,0:T(8,128)S(1)} fusion(bf16[16,32,1,128]{3,2,1,0:T(2,128)(2,1)S(1)} %get-tuple-element.9, bf16[16,32,128]{2,1,0:T(8,128)(2,1)S(1)} %bitcast.103, bf16[16,32,128]{2,1,0:T(8,128)(2,1)S(1)} %bitcast.111, bf16[16,32,128]{2,1,0:T(8,128)(2,1)S(1)} %bitcast.95, s32[16,32]{1,0:T(8,128)S(1)} %eq.34, s32[16,96]{1,0:T(8,128)S(1)} %get-tuple-element.30, ...), kind=kOutput, calls=%fused_computation.82 | convolution fusion | flops 14303327 | bytes 542720 | tf_op jit(solution)/shard_map/sub | solution.py:40
  29.2 0.5 fusion.11
  29.7 1.4 %fusion.55 = f32[16,32]{1,0:T(8,128)S(1)} fusion(bf16[16,32,1,128]{3,2,1,0:T(2,128)(2,1)S(1)} %get-tuple-element.7, bf16[16,32,128]{2,1,0:T(8,128)(2,1)S(1)} %bitcast.105, bf16[16,32,128]{2,1,0:T(8,128)(2,1)S(1)} %bitcast.113, bf16[16,32,128]{2,1,0:T(8,128)(2,1)S(1)} %bitcast.97, s32[16,32]{1,0:T(8,128)S(1)} %eq.34, s32[16,96]{1,0:T(8,128)S(1)} %get-tuple-element.30, ...), kind=kOutput, calls=%fused_computation.83 | convolution fusion | flops 14303327 | bytes 542720 | tf_op jit(solution)/shard_map/sub | solution.py:40
  31.1 0.5 fusion.12
  31.5 1.1 %fusion.24 = bf16[16,32,128]{2,1,0:T(8,128)(2,1)S(1)} fusion(f32[16,32]{1,0:T(8,128)S(1)} %fusion.52, f32[16,32,96]{2,1,0:T(8,128)S(1)} %fusion.9, bf16[16,32,128]{2,1,0:T(8,128)(2,1)S(1)} %bitcast.83, bf16[16,32,128]{2,1,0:T(8,128)(2,1)S(1)} %bitcast.87, bf16[16,32,128]{2,1,0:T(8,128)(2,1)S(1)} %bitcast.79, s32[16,32]{1,0:T(8,128)S(1)} %eq.34, ...), kind=kOutput, calls=%fused_computation.34 | convolution fusion | flops 14189151 | bytes 739328 | tf_op jit(solution)/shard_map/fkm,fmp->fkp/dot_general | solution.py:42
  32.6 1.1 %fusion.23 = bf16[16,32,128]{2,1,0:T(8,128)(2,1)S(1)} fusion(f32[16,32]{1,0:T(8,128)S(1)} %fusion.53, f32[16,32,96]{2,1,0:T(8,128)S(1)} %fusion.10, bf16[16,32,128]{2,1,0:T(8,128)(2,1)S(1)} %bitcast.84, bf16[16,32,128]{2,1,0:T(8,128)(2,1)S(1)} %bitcast.88, bf16[16,32,128]{2,1,0:T(8,128)(2,1)S(1)} %bitcast.80, s32[16,32]{1,0:T(8,128)S(1)} %eq.34, ...), kind=kOutput, calls=%fused_computation.33 | convolution fusion | flops 14189151 | bytes 739328 | tf_op jit(solution)/shard_map/fkm,fmp->fkp/dot_general | solution.py:42
  33.7 1.1 %fusion.22 = bf16[16,32,128]{2,1,0:T(8,128)(2,1)S(1)} fusion(f32[16,32]{1,0:T(8,128)S(1)} %fusion.54, f32[16,32,96]{2,1,0:T(8,128)S(1)} %fusion.11, bf16[16,32,128]{2,1,0:T(8,128)(2,1)S(1)} %bitcast.85, bf16[16,32,128]{2,1,0:T(8,128)(2,1)S(1)} %bitcast.89, bf16[16,32,128]{2,1,0:T(8,128)(2,1)S(1)} %bitcast.81, s32[16,32]{1,0:T(8,128)S(1)} %eq.34, ...), kind=kOutput, calls=%fused_computation.32 | convolution fusion | flops 14189151 | bytes 739328 | tf_op jit(solution)/shard_map/fkm,fmp->fkp/dot_general | solution.py:42
  34.8 1.1 %fusion.21 = bf16[16,32,128]{2,1,0:T(8,128)(2,1)S(1)} fusion(f32[16,32]{1,0:T(8,128)S(1)} %fusion.55, f32[16,32,96]{2,1,0:T(8,128)S(1)} %fusion.12, bf16[16,32,128]{2,1,0:T(8,128)(2,1)S(1)} %bitcast.86, bf16[16,32,128]{2,1,0:T(8,128)(2,1)S(1)} %bitcast.90, bf16[16,32,128]{2,1,0:T(8,128)(2,1)S(1)} %bitcast.82, s32[16,32]{1,0:T(8,128)S(1)} %eq.34, ...), kind=kOutput, calls=%fused_computation.31 | convolution fusion | flops 14189151 | bytes 739328 | tf_op jit(solution)/shard_map/fkm,fmp->fkp/dot_general | solution.py:42
  36.0 0.5 %broadcast.56 = bf16[]{:T(256)} broadcast(bf16[]{:T(256)} %constant.148), dimensions={} | broadcast | bytes 4 | tf_op jit(solution)/shard_map/reshape | solution.py:123
  36.5 1.0 %reduce = bf16[512,512]{1,0:T(8,128)(2,1)S(1)} reduce(bf16[512,1,512]{2,0,1:T(8,128)(2,1)S(1)} %bitcast.70, bf16[]{:T(256)} %broadcast.56), dimensions={1}, to_apply=%copy.36.reduce_sub_computation | reduce | bytes 1048578 | tf_op jit(solution)/shard_map/reshape | solution.py:123
  37.5 0.4 reshape.90
  37.9 11.2 %all_to_all.48 = bf16[4,2,32768]{2,1,0:T(2,128)(2,1)S(1)} all-to-all(bf16[4,2,32768]{2,1,0:T(2,128)(2,1)S(1)} %reshape.90), channel_id=1, replica_groups=mesh['ctx'=8,'head'=4] {'head'}, dimensions={0} | all-to-all | bytes 1048576 | tf_op jit(solution)/shard_map/all_to_all | solution.py:124
  49.1 0.5 %reshape.91 = bf16[512,1,512]{2,1,0:T(2,128)(2,1)S(1)} reshape(bf16[4,2,32768]{2,1,0:T(2,128)(2,1)S(1)} %all_to_all.48) | data formatting | bytes 1048576
  49.6 0.1 copy.40
  49.8 0.5 convolution_convert_fusion
  50.3 0.9 %copy.45 = bf16[16,8,4,512]{3,1,2,0:T(8,128)(2,1)} copy(bf16[16,8,4,512]{3,2,1,0:T(4,128)(2,1)S(1)} %bitcast.75) | data formatting | bytes 1048576
  (18 shorter events, 0.4 us)
Async XLA Ops:
  0.0 1.0 %copy-start.1 = (bf16[128,256]{1,0:T(8,128)(2,1)S(1)}, bf16[128,256]{1,0:T(8,128)(2,1)}, u32[]{:S(2)}) copy-start(bf16[128,256]{1,0:T(8,128)(2,1)} %param.6) | copy-start | bytes 196612
  0.0 6.0 %copy-start = (bf16[128,2048]{1,0:T(8,128)(2,1)S(1)}, bf16[128,2048]{1,0:T(8,128)(2,1)}, u32[]{:S(2)}) copy-start(bf16[128,2048]{1,0:T(8,128)(2,1)} %param.5) | copy-start | bytes 1572868
  1.8 8.8 %all-to-all-start.1 = ((bf16[128,4,128]{0,2,1:T(8,128)(2,1)}), bf16[128,4,128]{0,2,1:T(8,128)(2,1)S(1)}, u32[]{:S(2)}, u32[]{:S(2)}) async-start(bf16[128,4,128]{0,2,1:T(8,128)(2,1)} %pad_maximum_fusion.4), calls=%async_computation.1 | async-start | bytes 262144 | tf_op jit(solution)/shard_map/all_to_all | solution.py:82
  6.5 0.7 %copy-start.3 = (s32[4]{0:T(128)S(1)}, s32[4]{0:T(128)}, u32[]{:S(2)}) copy-start(s32[4]{0:T(128)} %param.8) | copy-start | bytes 52
  7.9 0.7 %copy-start.2 = (s32[4096]{0:T(1024)S(1)}, s32[4096]{0:T(1024)}, u32[]{:S(2)}) copy-start(s32[4096]{0:T(1024)} %param.9) | copy-start | bytes 49156
  10.6 12.3 %all-to-all-start = ((bf16[128,4,512]{2,0,1:T(8,128)(2,1)}), bf16[128,4,512]{2,0,1:T(8,128)(2,1)S(1)}, u32[]{:S(2)}, u32[]{:S(2)}) async-start(bf16[128,4,512]{2,0,1:T(8,128)(2,1)} %copy.28), calls=%async_computation | async-start | bytes 1048576 | tf_op jit(solution)/shard_map/all_to_all | solution.py:81
  14.3 5.4 %collective-permute-start = (bf16[64,128]{1,0:T(8,128)(2,1)S(1)}, bf16[64,128]{1,0:T(8,128)(2,1)S(1)}, u32[]{:S(2)}, u32[]{:S(2)}) collective-permute-start(bf16[64,128]{1,0:T(8,128)(2,1)S(1)} %slice.154), channel_id=1, source_target_pairs={{0,4},{4,8},{8,12},{12,16},{16,20},{20,24},{24,28},{1,5},{5,9},{9,... | collective-permute-start | bytes 49160 | tf_op jit(solution)/shard_map/ppermute | solution.py:15
  19.7 1.4 %collective-permute-start.1 = (bf16[576,128]{1,0:T(8,128)(2,1)S(1)}, bf16[576,128]{1,0:T(8,128)(2,1)S(1)}, u32[]{:S(2)}, u32[]{:S(2)}) collective-permute-start(bf16[576,128]{1,0:T(8,128)(2,1)S(1)} %pad_maximum_fusion.3), channel_id=1, source_target_pairs={{0,1},{1,0},{2,3},{3,2},{4,5},{5,4},{6,7},{7,6},{8,9},{9,8},{10,11... | collective-permute-start | bytes 442376 | tf_op jit(solution)/shard_map/ppermute | solution.py:19
where the time goes:
time: 51.6 us; the launch traced here: 51.2 us
  matrix products  12.7 us (25%)
  starting transfers between devices  11.7 us (23%)
  blocking collectives  11.2 us (22%)
  local copies, waits for them, and re-layouts  7.82 us (15%)
  waiting for transfers between devices  4.42 us (9%)
  other arithmetic  3.04 us (6%)
    all_to_all x1, blocking collectives, on_device(): lax.all_to_all(result, 'head', split_axis=0, concat_axis=1, tiled=True)  11.2 us
    sub x4, matrix products, attend(): expo = jnp.where(visible, jnp.exp(scores - peak), 0.0)  5.47 us
    dot_general x4, matrix products, attend(): jnp.einsum('fkm,fmp->fkp', expo.astype(jnp.bfloat16), value_window, prefe...  4.35 us
    all_to_all x1, starting transfers between devices, on_device(): lax.all_to_all(pieces, 'head', split_axis=1, concat_axis=0, tiled=True)  4.24 us
    ppermute x1, starting transfers between devices, passed_along(): return lax.ppermute(array, axis, pairs)  3.96 us
    unnamed x14, local copies, waits for them, and re-layouts  3.88 us
    all_to_all x1, starting transfers between devices, on_device(): lax.all_to_all(grouped, 'head', split_axis=1, concat_axis=0, tiled=True)  3.47 us
    dot_general x4, matrix products, attend(): jnp.einsum('nhs,nos->nho', query_tile[:, :, head_index], key_window, pref...  1.84 us
  transfers between devices with their start and end apart: 4, of which 4 were waited for; matrix products, arithmetic and copies ran while one was open for 8% of the time, Pallas kernels for 0%

commit v1 on v0

--- a/solution.py
+++ b/solution.py
@@ -121,7 +121,10 @@
         key_doc_windows,
     )
     result = result.reshape(tok_dev, 1, width)
-    returned = lax.all_to_all(result, "head", split_axis=0, concat_axis=1, tiled=True)
+    size = lax.axis_size("head")
+    blocks = jnp.stack(jnp.split(result, size, axis=0), axis=0)
+    blocks = lax.all_to_all(blocks, "head", split_axis=0, concat_axis=0)
+    returned = jnp.concatenate(blocks, axis=1)
     returned = jnp.einsum(
         "sg,rsw->rgw", reorder, returned, preferred_element_type=jnp.float32
     ).astype(jnp.bfloat16)

time: 51.6 us -> 49.1 us (0.952)
  local copies, waits for them, and re-layouts: 7.82 us -> 6.32 us
  other arithmetic: 3.04 us -> 2.08 us
    reshape x1 -> x0, other arithmetic: 1.03 us -> none  [on_device(): result = result.reshape(tok_dev, 1, width)]
    unnamed x14 -> x11, local copies, waits for them, and re-layouts: 3.88 us -> 2.86 us
where the time goes in v1:
time: 49.1 us; the launch traced here: 48.7 us
  matrix products  12.7 us (26%)
  starting transfers between devices  11.7 us (24%)
  blocking collectives  11.2 us (23%)
  local copies, waits for them, and re-layouts  6.32 us (13%)
  waiting for transfers between devices  4.42 us (9%)
  other arithmetic  2.08 us (4%)
    all_to_all x1, blocking collectives, on_device(): blocks = lax.all_to_all(blocks, 'head', split_axis=0, concat_axis=0)  11.2 us
    sub x4, matrix products, attend(): expo = jnp.where(visible, jnp.exp(scores - peak), 0.0)  5.47 us
    dot_general x4, matrix products, attend(): jnp.einsum('fkm,fmp->fkp', expo.astype(jnp.bfloat16), value_window, prefe...  4.35 us
    all_to_all x1, starting transfers between devices, on_device(): lax.all_to_all(pieces, 'head', split_axis=1, concat_axis=0, tiled=True)  4.24 us
    ppermute x1, starting transfers between devices, passed_along(): return lax.ppermute(array, axis, pairs)  3.96 us
    all_to_all x1, starting transfers between devices, on_device(): lax.all_to_all(grouped, 'head', split_axis=1, concat_axis=0, tiled=True)  3.47 us
    unnamed x11, local copies, waits for them, and re-layouts  2.86 us
    dot_general x4, matrix products, attend(): jnp.einsum('nhs,nos->nho', query_tile[:, :, head_index], key_window, pref...  1.84 us
  transfers between devices with their start and end apart: 4, of which 4 were waited for; matrix products, arithmetic and copies ran while one was open for 8% of the time, Pallas kernels for 0%

profile of v1, /device:TPU:0, one launch (start us, length us, event | category | flops | bytes accessed | tf_op | source)
XLA Modules:
  0.0 48.7 jit_solution(7025890999256477015)
XLA Ops:
  0.0 1.0 %copy.41 = bf16[128,256]{0,1:T(8,128)(2,1)S(1)} copy(bf16[128,256]{1,0:T(8,128)(2,1)} %param.7) | data formatting | bytes 131072 | tf_op args[2]
  1.0 0.1 copy.40
  1.1 0.7 %pad_maximum_fusion.5 = bf16[128,4,128]{0,2,1:T(8,128)(2,1)} fusion(bf16[128,4,64]{0,2,1:T(8,128)(2,1)S(1)} %bitcast.81, bf16[128,4,64]{0,2,1:T(8,128)(2,1)S(1)} %bitcast.82), kind=kLoop, calls=%fused_computation.49 | loop fusion | flops 262144 | bytes 262144 | tf_op jit(solution)/shard_map/concatenate | solution.py:79
  1.8 4.2 %all-to-all-start.1 = ((bf16[128,4,128]{0,2,1:T(8,128)(2,1)}), bf16[128,4,128]{0,2,1:T(8,128)(2,1)S(1)}, u32[]{:S(2)}, u32[]{:S(2)}) async-start(bf16[128,4,128]{0,2,1:T(8,128)(2,1)} %pad_maximum_fusion.5), calls=%async_computation.1 | async-start | bytes 262144 | tf_op jit(solution)/shard_map/all_to_all | solution.py:82
  6.0 0.4 reshape.95
  6.5 0.6 %copy-done.3 = s32[4]{0:T(128)S(1)} copy-done((s32[4]{0:T(128)S(1)}, s32[4]{0:T(128)}, u32[]{:S(2)}) %copy-start.3) | copy-done | bytes 40
  7.1 0.7 %sort.17 = (s32[4]{0:T(128)}, s32[4]{0:T(128)S(1)}) sort(s32[4]{0:T(128)S(1)} %copy-done.3, s32[4]{0:T(128)S(1)} %iota.54), dimensions={0}, to_apply=%region_0.0 | sort | flops 8 | bytes 64 | tf_op jit(solution)/shard_map/jit(argsort)/sort | solution.py:70
  7.9 0.5 %fusion.4 = bf16[128,4,512]{2,1,0:T(4,128)(2,1)S(1)} fusion(bf16[128,4,512]{2,1,0:T(4,128)(2,1)S(1)} %reshape.95, s32[4]{0:T(128)S(1)} %get-tuple-element.6), kind=kOutput, calls=%fused_computation.6 | convolution fusion | flops 2359312 | bytes 1048592 | tf_op jit(solution)/shard_map/sg,rgw->rsw/dot_general | solution.py:74
  8.4 0.2 copy-done.2
  8.6 0.1 pad_dynamic-slice_fusion
  8.7 0.1 fusion.52
  8.7 0.9 %copy.38 = bf16[128,4,512]{2,0,1:T(8,128)(2,1)} copy(bf16[128,4,512]{2,1,0:T(4,128)(2,1)S(1)} %fusion.4) | data formatting | bytes 1048576 | tf_op jit(solution)/shard_map/convert_element_type | solution.py:76
  9.6 0.1 slice.132
  9.7 0.1 slice.130
  9.8 0.1 slice.128
  9.8 0.8 %all-to-all-done.1 = bf16[128,4,128]{0,2,1:T(8,128)(2,1)S(1)} async-done(((bf16[128,4,128]{0,2,1:T(8,128)(2,1)}), bf16[128,4,128]{0,2,1:T(8,128)(2,1)S(1)}, u32[]{:S(2)}, u32[]{:S(2)}) %all-to-all-start.1) | async-done | bytes 131104 | tf_op jit(solution)/shard_map/all_to_all | solution.py:82
  10.6 3.5 %all-to-all-start = ((bf16[128,4,512]{2,0,1:T(8,128)(2,1)}), bf16[128,4,512]{2,0,1:T(8,128)(2,1)S(1)}, u32[]{:S(2)}, u32[]{:S(2)}) async-start(bf16[128,4,512]{2,0,1:T(8,128)(2,1)} %copy.38), calls=%async_computation | async-start | bytes 1048576 | tf_op jit(solution)/shard_map/all_to_all | solution.py:81
  14.1 0.1 copy.42
  14.3 4.0 %collective-permute-start = (bf16[64,128]{1,0:T(8,128)(2,1)S(1)}, bf16[64,128]{1,0:T(8,128)(2,1)S(1)}, u32[]{:S(2)}, u32[]{:S(2)}) collective-permute-start(bf16[64,128]{1,0:T(8,128)(2,1)S(1)} %slice.158), channel_id=1, source_target_pairs={{0,4},{4,8},{8,12},{12,16},{16,20},{20,24},{24,28},{1,5},{5,9},{9,... | collective-permute-start | bytes 49160 | tf_op jit(solution)/shard_map/ppermute | solution.py:15
  18.2 0.1 pad_add_fusion
  18.3 1.3 %collective-permute-done = bf16[64,128]{1,0:T(8,128)(2,1)S(1)} collective-permute-done((bf16[64,128]{1,0:T(8,128)(2,1)S(1)}, bf16[64,128]{1,0:T(8,128)(2,1)S(1)}, u32[]{:S(2)}, u32[]{:S(2)}) %collective-permute-start) | collective-permute-done | bytes 16416 | tf_op jit(solution)/shard_map/ppermute | solution.py:15
  19.7 0.1 collective-permute-start.1
  19.8 0.1 dynamic_slice.7
  19.9 0.1 eq.34
  19.9 0.1 fusion.28
  20.1 1.1 %collective-permute-done.1 = bf16[576,128]{1,0:T(8,128)(2,1)S(1)} collective-permute-done((bf16[576,128]{1,0:T(8,128)(2,1)S(1)}, bf16[576,128]{1,0:T(8,128)(2,1)S(1)}, u32[]{:S(2)}, u32[]{:S(2)}) %collective-permute-start.1) | collective-permute-done | bytes 147488 | tf_op jit(solution)/shard_map/ppermute | solution.py:19
  21.1 0.1 fusion.49
  21.2 0.3 maximum_select_fusion
  21.7 1.2 %all-to-all-done = bf16[128,4,512]{2,0,1:T(8,128)(2,1)S(1)} async-done(((bf16[128,4,512]{2,0,1:T(8,128)(2,1)}), bf16[128,4,512]{2,0,1:T(8,128)(2,1)S(1)}, u32[]{:S(2)}, u32[]{:S(2)}) %all-to-all-start) | async-done | bytes 524320 | tf_op jit(solution)/shard_map/all_to_all | solution.py:81
  22.9 0.1 reshape.96
  23.0 1.1 %fusion.47 = (bf16[16,32,1,128]{3,2,1,0:T(2,128)(2,1)S(1)}, bf16[16,32,1,128]{3,2,1,0:T(2,128)(2,1)S(1)}, bf16[16,32,1,128]{3,2,1,0:T(2,128)(2,1)S(1)}, bf16[16,32,1,128]{3,2,1,0:T(2,128)(2,1)S(1)}) fusion(bf16[16,32,4,128]{3,2,1,0:T(4,128)(2,1)S(1)} %reshape.96), kind=kLoop, calls=%fused_computation.76 | loop fusion | bytes 1048576 | tf_op jit(solution)/shard_map/slice | solution.py:32
  24.2 1.4 %fusion.53 = f32[16,32]{1,0:T(8,128)S(1)} fusion(bf16[16,32,1,128]{3,2,1,0:T(2,128)(2,1)S(1)} %get-tuple-element.14, bf16[16,32,128]{2,1,0:T(8,128)(2,1)S(1)} %bitcast.103, bf16[16,32,128]{2,1,0:T(8,128)(2,1)S(1)} %bitcast.111, bf16[16,32,128]{2,1,0:T(8,128)(2,1)S(1)} %bitcast.95, s32[16,32]{1,0:T(8,128)S(1)} %eq.34, s32[16,96]{1,0:T(8,128)S(1)} %get-tuple-element.34, ...), kind=kOutput, calls=%fused_computation.82 | convolution fusion | flops 14303327 | bytes 542720 | tf_op jit(solution)/shard_map/sub | solution.py:40
  25.5 0.5 fusion.9
  26.0 1.4 %fusion.54 = f32[16,32]{1,0:T(8,128)S(1)} fusion(bf16[16,32,1,128]{3,2,1,0:T(2,128)(2,1)S(1)} %get-tuple-element.12, bf16[16,32,128]{2,1,0:T(8,128)(2,1)S(1)} %bitcast.105, bf16[16,32,128]{2,1,0:T(8,128)(2,1)S(1)} %bitcast.113, bf16[16,32,128]{2,1,0:T(8,128)(2,1)S(1)} %bitcast.97, s32[16,32]{1,0:T(8,128)S(1)} %eq.34, s32[16,96]{1,0:T(8,128)S(1)} %get-tuple-element.34, ...), kind=kOutput, calls=%fused_computation.83 | convolution fusion | flops 14303327 | bytes 542720 | tf_op jit(solution)/shard_map/sub | solution.py:40
  27.4 0.5 fusion.10
  27.9 1.4 %fusion.55 = f32[16,32]{1,0:T(8,128)S(1)} fusion(bf16[16,32,1,128]{3,2,1,0:T(2,128)(2,1)S(1)} %get-tuple-element.13, bf16[16,32,128]{2,1,0:T(8,128)(2,1)S(1)} %bitcast.107, bf16[16,32,128]{2,1,0:T(8,128)(2,1)S(1)} %bitcast.115, bf16[16,32,128]{2,1,0:T(8,128)(2,1)S(1)} %bitcast.99, s32[16,32]{1,0:T(8,128)S(1)} %eq.34, s32[16,96]{1,0:T(8,128)S(1)} %get-tuple-element.34, ...), kind=kOutput, calls=%fused_computation.84 | convolution fusion | flops 14303327 | bytes 542720 | tf_op jit(solution)/shard_map/sub | solution.py:40
  29.2 0.5 fusion.11
  29.7 1.4 %fusion.56 = f32[16,32]{1,0:T(8,128)S(1)} fusion(bf16[16,32,1,128]{3,2,1,0:T(2,128)(2,1)S(1)} %get-tuple-element.11, bf16[16,32,128]{2,1,0:T(8,128)(2,1)S(1)} %bitcast.109, bf16[16,32,128]{2,1,0:T(8,128)(2,1)S(1)} %bitcast.117, bf16[16,32,128]{2,1,0:T(8,128)(2,1)S(1)} %bitcast.101, s32[16,32]{1,0:T(8,128)S(1)} %eq.34, s32[16,96]{1,0:T(8,128)S(1)} %get-tuple-element.34, ...), kind=kOutput, calls=%fused_computation.85 | convolution fusion | flops 14303327 | bytes 542720 | tf_op jit(solution)/shard_map/sub | solution.py:40
  31.1 0.5 fusion.12
  31.5 1.1 %fusion.24 = bf16[16,32,128]{2,1,0:T(8,128)(2,1)S(1)} fusion(f32[16,32]{1,0:T(8,128)S(1)} %fusion.53, f32[16,32,96]{2,1,0:T(8,128)S(1)} %fusion.9, bf16[16,32,128]{2,1,0:T(8,128)(2,1)S(1)} %bitcast.87, bf16[16,32,128]{2,1,0:T(8,128)(2,1)S(1)} %bitcast.91, bf16[16,32,128]{2,1,0:T(8,128)(2,1)S(1)} %bitcast.83, s32[16,32]{1,0:T(8,128)S(1)} %eq.34, ...), kind=kOutput, calls=%fused_computation.34 | convolution fusion | flops 14189151 | bytes 739328 | tf_op jit(solution)/shard_map/fkm,fmp->fkp/dot_general | solution.py:42
  32.6 1.1 %fusion.23 = bf16[16,32,128]{2,1,0:T(8,128)(2,1)S(1)} fusion(f32[16,32]{1,0:T(8,128)S(1)} %fusion.54, f32[16,32,96]{2,1,0:T(8,128)S(1)} %fusion.10, bf16[16,32,128]{2,1,0:T(8,128)(2,1)S(1)} %bitcast.88, bf16[16,32,128]{2,1,0:T(8,128)(2,1)S(1)} %bitcast.92, bf16[16,32,128]{2,1,0:T(8,128)(2,1)S(1)} %bitcast.84, s32[16,32]{1,0:T(8,128)S(1)} %eq.34, ...), kind=kOutput, calls=%fused_computation.33 | convolution fusion | flops 14189151 | bytes 739328 | tf_op jit(solution)/shard_map/fkm,fmp->fkp/dot_general | solution.py:42
  33.7 1.1 %fusion.22 = bf16[16,32,128]{2,1,0:T(8,128)(2,1)S(1)} fusion(f32[16,32]{1,0:T(8,128)S(1)} %fusion.55, f32[16,32,96]{2,1,0:T(8,128)S(1)} %fusion.11, bf16[16,32,128]{2,1,0:T(8,128)(2,1)S(1)} %bitcast.89, bf16[16,32,128]{2,1,0:T(8,128)(2,1)S(1)} %bitcast.93, bf16[16,32,128]{2,1,0:T(8,128)(2,1)S(1)} %bitcast.85, s32[16,32]{1,0:T(8,128)S(1)} %eq.34, ...), kind=kOutput, calls=%fused_computation.32 | convolution fusion | flops 14189151 | bytes 739328 | tf_op jit(solution)/shard_map/fkm,fmp->fkp/dot_general | solution.py:42
  34.8 1.1 %fusion.21 = bf16[16,32,128]{2,1,0:T(8,128)(2,1)S(1)} fusion(f32[16,32]{1,0:T(8,128)S(1)} %fusion.56, f32[16,32,96]{2,1,0:T(8,128)S(1)} %fusion.12, bf16[16,32,128]{2,1,0:T(8,128)(2,1)S(1)} %bitcast.90, bf16[16,32,128]{2,1,0:T(8,128)(2,1)S(1)} %bitcast.94, bf16[16,32,128]{2,1,0:T(8,128)(2,1)S(1)} %bitcast.86, s32[16,32]{1,0:T(8,128)S(1)} %eq.34, ...), kind=kOutput, calls=%fused_computation.31 | convolution fusion | flops 14189151 | bytes 739328 | tf_op jit(solution)/shard_map/fkm,fmp->fkp/dot_general | solution.py:42
  35.9 0.1 pad_maximum_fusion
  36.0 0.1 pad_maximum_fusion.1
  36.1 11.2 %all_to_all.35 = bf16[4,128,1,512]{3,1,2,0:T(8,128)(2,1)S(1)} all-to-all(bf16[4,128,1,512]{3,1,2,0:T(8,128)(2,1)S(1)} %pad_maximum_fusion.1), channel_id=1, replica_groups=mesh['ctx'=8,'head'=4] {'head'}, dimensions={0} | all-to-all | bytes 1048576 | tf_op jit(solution)/shard_map/all_to_all | solution.py:126
  47.3 0.5 %convolution_convert_fusion = bf16[128,512,4]{1,2,0:T(4,128)(2,1)S(1)} fusion(bf16[4,128,1,512]{3,1,2,0:T(8,128)(2,1)S(1)} %all_to_all.35, s32[4]{0:T(128)S(1)} %get-tuple-element.6), kind=kOutput, calls=%fused_computation.4 | convolution fusion | flops 2359312 | bytes 1048592 | tf_op jit(solution)/shard_map/sg,rsw->rgw/dot_general | solution.py:128
  47.8 0.9 %copy.53 = bf16[16,8,4,512]{3,1,2,0:T(8,128)(2,1)} copy(bf16[16,8,4,512]{3,2,1,0:T(4,128)(2,1)S(1)} %bitcast.75) | data formatting | bytes 1048576
  (15 shorter events, 0.2 us)
Async XLA Ops:
  0.0 1.0 %copy-start.1 = (bf16[128,256]{1,0:T(8,128)(2,1)S(1)}, bf16[128,256]{1,0:T(8,128)(2,1)}, u32[]{:S(2)}) copy-start(bf16[128,256]{1,0:T(8,128)(2,1)} %param.6) | copy-start | bytes 196612
  0.0 6.0 %copy-start = (bf16[128,2048]{1,0:T(8,128)(2,1)S(1)}, bf16[128,2048]{1,0:T(8,128)(2,1)}, u32[]{:S(2)}) copy-start(bf16[128,2048]{1,0:T(8,128)(2,1)} %param.5) | copy-start | bytes 1572868
  1.8 8.8 %all-to-all-start.1 = ((bf16[128,4,128]{0,2,1:T(8,128)(2,1)}), bf16[128,4,128]{0,2,1:T(8,128)(2,1)S(1)}, u32[]{:S(2)}, u32[]{:S(2)}) async-start(bf16[128,4,128]{0,2,1:T(8,128)(2,1)} %pad_maximum_fusion.5), calls=%async_computation.1 | async-start | bytes 262144 | tf_op jit(solution)/shard_map/all_to_all | solution.py:82
  6.5 0.7 %copy-start.3 = (s32[4]{0:T(128)S(1)}, s32[4]{0:T(128)}, u32[]{:S(2)}) copy-start(s32[4]{0:T(128)} %param.8) | copy-start | bytes 52
  7.9 0.7 %copy-start.2 = (s32[4096]{0:T(1024)S(1)}, s32[4096]{0:T(1024)}, u32[]{:S(2)}) copy-start(s32[4096]{0:T(1024)} %param.9) | copy-start | bytes 49156
  10.6 12.3 %all-to-all-start = ((bf16[128,4,512]{2,0,1:T(8,128)(2,1)}), bf16[128,4,512]{2,0,1:T(8,128)(2,1)S(1)}, u32[]{:S(2)}, u32[]{:S(2)}) async-start(bf16[128,4,512]{2,0,1:T(8,128)(2,1)} %copy.38), calls=%async_computation | async-start | bytes 1048576 | tf_op jit(solution)/shard_map/all_to_all | solution.py:81
  14.3 5.4 %collective-permute-start = (bf16[64,128]{1,0:T(8,128)(2,1)S(1)}, bf16[64,128]{1,0:T(8,128)(2,1)S(1)}, u32[]{:S(2)}, u32[]{:S(2)}) collective-permute-start(bf16[64,128]{1,0:T(8,128)(2,1)S(1)} %slice.158), channel_id=1, source_target_pairs={{0,4},{4,8},{8,12},{12,16},{16,20},{20,24},{24,28},{1,5},{5,9},{9,... | collective-permute-start | bytes 49160 | tf_op jit(solution)/shard_map/ppermute | solution.py:15
  19.7 1.4 %collective-permute-start.1 = (bf16[576,128]{1,0:T(8,128)(2,1)S(1)}, bf16[576,128]{1,0:T(8,128)(2,1)S(1)}, u32[]{:S(2)}, u32[]{:S(2)}) collective-permute-start(bf16[576,128]{1,0:T(8,128)(2,1)S(1)} %pad_maximum_fusion.4), channel_id=1, source_target_pairs={{0,1},{1,0},{2,3},{3,2},{4,5},{5,4},{6,7},{7,6},{8,9},{9,8},{10,11... | collective-permute-start | bytes 442376 | tf_op jit(solution)/shard_map/ppermute | solution.py:19
